TPU v7x, 128 devices: a whole 4x4x4 slice. The times are simulated.
128 devices in a mesh: row: 8 (over z, core), col: 16 (over x, y).
Axes of the slice: x: 4, y: 4, z: 4, core: 2. Of those that a mesh axis runs over, the one named last changes fastest.
Arguments:
- hessian_inverse: float32 [12288, 12288], P('row', 'col'), as said below
- weight: bfloat16 [12288, 4096], P('row', 'col'), may hold values from -6 to 6
- pruned: int32 [2, 512], replicated, may hold values from 0 to 12287, as said below
Outputs:
- hessian_after: float32 [12288, 12288], P('row', 'col')
- weight_after: bfloat16 [12288, 4096], P('row', 'col')
Inputs may be any that keep to these rules, and one draw needn't show every extreme that they name: `hessian_inverse`: symmetric and positive definite. `pruned`: all 1024 channel numbers are distinct.
All inputs are finite; a program needn't handle non-finite values.
Results may differ from a plain program's by a relative error of at most 0.001.
Values sent between devices are 32-bit elements; how exact they have to be, the bound alone decides.
No kernel may reach another device: no remote copies, remote signals or barrier semaphores. Data moves between devices by JAX's collectives and lax.ppermute only.
A program may use at most 128 MiB of HBM per device.

v0:
```python
import jax
import jax.numpy as jnp
from jax import lax
from jax.sharding import PartitionSpec as P

PANELS = 2


def contract_rows(gains, rows):
    return lax.dot_general(
        gains,
        rows,
        (((0,), (0,)), ((), ())),
        precision=lax.Precision.HIGHEST,
        preferred_element_type=jnp.float32,
    )


def solve_pivot(factor, rhs):
    half = lax.linalg.triangular_solve(factor, rhs, left_side=True, lower=True)
    return lax.linalg.triangular_solve(factor, half, left_side=True, lower=True, transpose_a=True)


def locate(listed, start, count):
    local_ids = listed - start
    valid = (local_ids >= 0) & (local_ids < count)
    clipped = jnp.clip(local_ids, 0, count - 1)
    marked = jnp.zeros((count,), jnp.float32).at[clipped].max(valid.astype(jnp.float32)) > 0.5
    return (clipped, valid, marked)


def per_device(hessian_inverse, weight, pruned):
    row_count = hessian_inverse.shape[0]
    col_count = hessian_inverse.shape[1]
    row_start = lax.axis_index("row") * row_count
    col_start = lax.axis_index("col") * col_count
    inverse = hessian_inverse
    slab = weight.astype(jnp.float32)
    for panel in range(PANELS):
        listed = pruned[panel]
        row_pick, row_valid, row_marked = locate(listed, row_start, row_count)
        col_pick, col_valid, col_marked = locate(listed, col_start, col_count)
        mine_rows = jnp.where(row_valid[:, None], jnp.take(inverse, row_pick, axis=0), 0.0)
        mine_slab = jnp.where(row_valid[:, None], jnp.take(slab, row_pick, axis=0), 0.0)
        panel_rows, slab_rows = lax.psum((mine_rows, mine_slab), "row")
        panel_pivot = jnp.where(col_valid[None, :], jnp.take(panel_rows, col_pick, axis=1), 0.0)
        pivot = lax.psum(panel_pivot, "col")
        factor = jnp.linalg.cholesky(pivot)
        mine_cols = jnp.where(col_valid[None, :], jnp.take(inverse, col_pick, axis=1), 0.0)
        columns = lax.psum(mine_cols, "col")
        gains = solve_pivot(factor, columns.T)
        slab = slab - contract_rows(gains, slab_rows)
        slab = jnp.where(row_marked[:, None], 0.0, slab)
        inverse = inverse - contract_rows(gains, panel_rows)
        inverse = jnp.where(row_marked[:, None] | col_marked[None, :], 0.0, inverse)
    return (inverse, slab.astype(jnp.bfloat16))


def solution(mesh):
    in_specs = (P("row", "col"), P("row", "col"), P())
    out_specs = (P("row", "col"), P("row", "col"))
    return jax.shard_map(
        per_device, mesh=mesh, in_specs=in_specs, out_specs=out_specs, check_vma=False
    )
```

profile of v0, /device:TPU:1, one launch (start us, length us, event | category | flops | bytes accessed | tf_op | source)
XLA Modules:
  0.0 719.2 jit_solution(886581179572580454)
XLA Ops:
  10.1 4.8 gather_fusion
  14.9 2.2 gather_fusion.6
  19.7 6.0 copy.13
  25.7 6.0 gather_fusion.2
  31.7 2.1 fusion.1
  33.8 53.3 %all-reduce.16.cloned.1.call-done = (f32[512,768]{1,0:T(8,128)}, f32[512,256]{1,0:T(8,128)}) async-done(((f32[512,768]{1,0:T(8,128)}, f32[512,256]{1,0:T(8,128)}), (f32[512,768]{1,0:T(8,128)}, f32[512,256]{1,0:T(8,128)})) %all-reduce.16.cloned.1.call-update) | async-done | bytes 2097168 | tf_op jit(solution)/shard_map/psum | solution.py:45
  87.1 1.9 copy.11
  91.9 4.1 scatter_custom_fusion.3
  96.0 3.7 scatter_custom_fusion.2
  99.8 96.6 %all-reduce.12.cloned.1.call-done = (f32[512,1536]{1,0:T(8,128)}, f32[512,512]{0,1:T(8,128)}) async-done(((f32[512,1536]{1,0:T(8,128)}, f32[512,512]{0,1:T(8,128)}), (f32[512,1536]{1,0:T(8,128)}, f32[512,512]{0,1:T(8,128)})) %all-reduce.12.cloned.1.call-update) | async-done | bytes 4194320 | tf_op jit(solution)/shard_map/psum | solution.py:50
  198.3 11.7 %cholesky.286 = f32[128,128]{1,0:T(8,128)S(1)} custom-call(f32[128,128]{1,0:T(8,128)S(1)} %cholesky.426), custom_call_target="Cholesky" | custom-call | tf_op jit(solution)/shard_map/jit(cholesky)/cholesky | solution.py:48
  210.2 9.8 %custom-call.31 = f32[1,128,128]{1,2,0:T(8,128)S(1)} custom-call(f32[1,128,128]{2,1,0:T(8,128)S(1)} %get-tuple-element.100), custom_call_target="InvertDiagBlocksLowerTriangular" | custom-call | tf_op jit(solution)/shard_map/jit(cholesky)/cholesky | solution.py:48
  220.6 11.7 %cholesky.305 = f32[128,128]{1,0:T(8,128)S(1)} custom-call(f32[128,128]{1,0:T(8,128)S(1)} %cholesky.430), custom_call_target="Cholesky" | custom-call | tf_op jit(solution)/shard_map/jit(cholesky)/cholesky | solution.py:48
  232.4 10.2 %custom-call.32 = f32[1,128,128]{1,2,0:T(8,128)S(1)} custom-call(f32[1,128,128]{2,1,0:T(8,128)S(1)} %get-tuple-element.97), custom_call_target="InvertDiagBlocksLowerTriangular" | custom-call | tf_op jit(solution)/shard_map/jit(cholesky)/cholesky | solution.py:48
  243.2 11.7 %cholesky.326 = f32[128,128]{1,0:T(8,128)S(1)} custom-call(f32[128,128]{1,0:T(8,128)S(1)} %cholesky.435), custom_call_target="Cholesky" | custom-call | tf_op jit(solution)/shard_map/jit(cholesky)/cholesky | solution.py:48
  255.0 9.8 %custom-call.33 = f32[1,128,128]{1,2,0:T(8,128)S(1)} custom-call(f32[1,128,128]{2,1,0:T(8,128)S(1)} %get-tuple-element.94), custom_call_target="InvertDiagBlocksLowerTriangular" | custom-call | tf_op jit(solution)/shard_map/jit(cholesky)/cholesky | solution.py:48
  265.4 11.7 %cholesky.343 = f32[128,128]{1,0:T(8,128)S(1)} custom-call(f32[128,128]{1,0:T(8,128)S(1)} %convolution_subtract_fusion.19), custom_call_target="Cholesky" | custom-call | tf_op jit(solution)/shard_map/jit(cholesky)/cholesky | solution.py:48
  282.0 7.6 %while.8 = (s32[]{:T(128)}, f32[512,512]{1,0:T(8,128)S(1)}, s32[4,2]{0,1:T(2,128)S(1)}, f32[4,128,128]{2,1,0:T(8,128)S(1)}, s32[]{:T(128)}) while((s32[]{:T(128)}, f32[512,512]{1,0:T(8,128)S(1)}, s32[4,2]{0,1:T(2,128)S(1)}, f32[4,128,128]{2,1,0:T(8,128)S(1)}, s32[]{:T(128)}) %tuple.80), condition=%wide.while_cond.1, body=%wide.while_body.1.sunk | while | flops 2 | bytes 131189 | solution.py:21
  289.6 39.3 %custom-call.35 = f32[4,128,128]{1,2,0:T(8,128)S(1)} custom-call(f32[4,128,128]{2,1,0:T(8,128)S(1)} %get-tuple-element.38), custom_call_target="InvertDiagBlocksLowerTriangular" | custom-call | tf_op jit(solution)/shard_map/triangular_solve/custom-call.8 | solution.py:21
  328.9 2.0 fusion.41
  330.9 2.1 convolution_subtract_fusion.13
  342.4 2.0 convolution_subtract_fusion.10
  345.3 10.7 %subtract_select_fusion.1 = f32[1536,768]{1,0:T(8,128)} fusion(f32[1536,768]{1,0:T(8,128)S(1)} %bitcast.167, f32[512,768]{1,0:T(8,128)S(1)} %copy-done.2, pred[768]{0:T(1024)(128)(4,1)S(1)} %broadcast_compare_fusion.2, pred[1536]{0:T(1024)(128)(4,1)S(1)} %broadcast_compare_fusion, f32[128,1536]{1,0:T(8,128)S(1)} %fusion.83, f32[128,1536]{1,0:T(8,128)S(1)} %fusion.81, ...), kind=kOutput, calls=%fused_computation.17 | convolution fusion | flops 7253655552 | bytes 14158080 | tf_op jit(solution)/shard_map/dot_general | solution.py:10
  356.0 5.5 fusion.3
  361.5 5.4 gather_fusion.3
  366.9 2.2 gather_fusion.7
  371.6 6.0 copy.16
  377.7 6.0 gather_fusion.5
  383.7 2.1 fusion
  385.8 50.2 %all-reduce.14.cloned.1.call-done = (f32[512,768]{1,0:T(8,128)}, f32[512,256]{1,0:T(8,128)}) async-done(((f32[512,768]{1,0:T(8,128)}, f32[512,256]{1,0:T(8,128)}), (f32[512,768]{1,0:T(8,128)}, f32[512,256]{1,0:T(8,128)})) %all-reduce.14.cloned.1.call-update) | async-done | bytes 2097168 | tf_op jit(solution)/shard_map/psum | solution.py:45
  436.0 1.9 copy.14
  440.7 4.1 scatter_custom_fusion.1
  444.8 3.7 scatter_custom_fusion
  448.5 96.7 %all-reduce.10.cloned.1.call-done = (f32[512,1536]{1,0:T(8,128)}, f32[512,512]{0,1:T(8,128)}) async-done(((f32[512,1536]{1,0:T(8,128)}, f32[512,512]{0,1:T(8,128)}), (f32[512,1536]{1,0:T(8,128)}, f32[512,512]{0,1:T(8,128)})) %all-reduce.10.cloned.1.call-update) | async-done | bytes 4194320 | tf_op jit(solution)/shard_map/psum | solution.py:50
  547.2 11.7 %cholesky.358 = f32[128,128]{1,0:T(8,128)S(1)} custom-call(f32[128,128]{1,0:T(8,128)S(1)} %cholesky.439), custom_call_target="Cholesky" | custom-call | tf_op jit(solution)/shard_map/jit(cholesky)/cholesky | solution.py:48
  559.0 9.8 %custom-call.36 = f32[1,128,128]{1,2,0:T(8,128)S(1)} custom-call(f32[1,128,128]{2,1,0:T(8,128)S(1)} %get-tuple-element.90), custom_call_target="InvertDiagBlocksLowerTriangular" | custom-call | tf_op jit(solution)/shard_map/jit(cholesky)/cholesky | solution.py:48
  569.5 11.7 %cholesky.377 = f32[128,128]{1,0:T(8,128)S(1)} custom-call(f32[128,128]{1,0:T(8,128)S(1)} %cholesky.443), custom_call_target="Cholesky" | custom-call | tf_op jit(solution)/shard_map/jit(cholesky)/cholesky | solution.py:48
  581.3 10.2 %custom-call.37 = f32[1,128,128]{1,2,0:T(8,128)S(1)} custom-call(f32[1,128,128]{2,1,0:T(8,128)S(1)} %get-tuple-element.87), custom_call_target="InvertDiagBlocksLowerTriangular" | custom-call | tf_op jit(solution)/shard_map/jit(cholesky)/cholesky | solution.py:48
  592.1 11.7 %cholesky.398 = f32[128,128]{1,0:T(8,128)S(1)} custom-call(f32[128,128]{1,0:T(8,128)S(1)} %cholesky.448), custom_call_target="Cholesky" | custom-call | tf_op jit(solution)/shard_map/jit(cholesky)/cholesky | solution.py:48
  603.9 9.8 %custom-call.38 = f32[1,128,128]{1,2,0:T(8,128)S(1)} custom-call(f32[1,128,128]{2,1,0:T(8,128)S(1)} %get-tuple-element.84), custom_call_target="InvertDiagBlocksLowerTriangular" | custom-call | tf_op jit(solution)/shard_map/jit(cholesky)/cholesky | solution.py:48
  614.3 11.7 %cholesky.415 = f32[128,128]{1,0:T(8,128)S(1)} custom-call(f32[128,128]{1,0:T(8,128)S(1)} %convolution_subtract_fusion.18), custom_call_target="Cholesky" | custom-call | tf_op jit(solution)/shard_map/jit(cholesky)/cholesky | solution.py:48
  631.7 8.1 %while.9 = (s32[]{:T(128)}, f32[512,512]{1,0:T(8,128)S(1)}, s32[4,2]{0,1:T(2,128)S(1)}, f32[4,128,128]{2,1,0:T(8,128)S(1)}, s32[]{:T(128)}) while((s32[]{:T(128)}, f32[512,512]{1,0:T(8,128)S(1)}, s32[4,2]{0,1:T(2,128)S(1)}, f32[4,128,128]{2,1,0:T(8,128)S(1)}, s32[]{:T(128)}) %tuple.98), condition=%wide.while_cond.1.clone, body=%wide.while_body.1.clone.sunk | while | flops 2 | bytes 131189 | solution.py:21
  639.8 39.3 %custom-call.40 = f32[4,128,128]{1,2,0:T(8,128)S(1)} custom-call(f32[4,128,128]{2,1,0:T(8,128)S(1)} %get-tuple-element.40), custom_call_target="InvertDiagBlocksLowerTriangular" | custom-call | tf_op jit(solution)/shard_map/triangular_solve/custom-call.8 | solution.py:21
  679.1 2.0 fusion.39
  681.1 2.1 convolution_subtract_fusion.9
  692.6 1.8 convolution_subtract_fusion.6
  695.3 10.7 %subtract_select_fusion = f32[1536,768]{1,0:T(8,128)} fusion(f32[1536,768]{1,0:T(8,128)S(1)} %bitcast.165, f32[512,768]{1,0:T(8,128)S(1)} %copy-done.3, pred[768]{0:T(1024)(128)(4,1)S(1)} %broadcast_compare_fusion.3, pred[1536]{0:T(1024)(128)(4,1)S(1)} %broadcast_compare_fusion.1, f32[128,1536]{1,0:T(8,128)S(1)} %fusion.90, f32[128,1536]{1,0:T(8,128)S(1)} %fusion.88, ...), kind=kOutput, calls=%fused_computation.16 | convolution fusion | flops 7253655552 | bytes 14158080 | tf_op jit(solution)/shard_map/dot_general | solution.py:10
  705.9 6.5 fusion.4
  (166 shorter events, 62.7 us)
Async XLA Ops:
  7.2 79.9 %all-reduce.16.cloned.1.call-start = ((), (), s32[]{:S(2)}) async-start(), calls=%async_computation.3 | async-start | bytes 4194304 | tf_op jit(solution)/shard_map/psum | solution.py:45
  17.2 1.4 copy-start.8
  19.6 176.8 %all-reduce.12.cloned.1.call-start = ((), (), s32[]{:S(2)}) async-start(), calls=%async_computation.1 | async-start | bytes 8388608 | tf_op jit(solution)/shard_map/psum | solution.py:50
  91.8 344.2 %all-reduce.14.cloned.1.call-start = ((), (), s32[]{:S(2)}) async-start(), calls=%async_computation.2 | async-start | bytes 4194304 | tf_op jit(solution)/shard_map/psum | solution.py:45
  196.4 1.7 copy-start.4
  330.9 2.9 copy-start.6
  338.2 7.0 slice-start.2
  340.6 4.6 slice-start.3
  342.4 2.8 copy-start.2
  345.2 10.7 %copy-start.10 = (bf16[1536,256]{1,0:T(8,128)(2,1)S(1)}, bf16[1536,256]{1,0:T(8,128)(2,1)}, u32[]{:S(2)}) copy-start(bf16[1536,256]{1,0:T(8,128)(2,1)} %param.17) | copy-start | bytes 2359300
  345.3 10.7 %copy-start.11 = (f32[512,256]{1,0:T(8,128)S(1)}, f32[512,256]{1,0:T(8,128)}, u32[]{:S(2)}) copy-start(f32[512,256]{1,0:T(8,128)} %get-tuple-element.68) | copy-start | bytes 1572868
  361.5 5.4 copy-start
  369.1 1.4 copy-start.9
  371.5 173.7 %all-reduce.10.cloned.1.call-start = ((), (), s32[]{:S(2)}) async-start(), calls=%async_computation | async-start | bytes 8388608 | tf_op jit(solution)/shard_map/psum | solution.py:50
  545.2 1.7 copy-start.5
  681.1 2.9 copy-start.7
  688.3 6.9 slice-start
  690.8 4.4 slice-start.1
  692.6 2.6 copy-start.3
  695.2 10.7 %copy-start.1 = (f32[1536,256]{1,0:T(8,128)S(1)}, f32[1536,256]{1,0:T(8,128)}, u32[]{:S(2)}) copy-start(f32[1536,256]{1,0:T(8,128)} %copy-done) | copy-start | bytes 4718596
  695.3 10.7 %copy-start.12 = (f32[512,256]{1,0:T(8,128)S(1)}, f32[512,256]{1,0:T(8,128)}, u32[]{:S(2)}) copy-start(f32[512,256]{1,0:T(8,128)} %get-tuple-element.66) | copy-start | bytes 1572868
Sparse Core Ops, SparseCore 0:
  19.7 67.3 all-reduce.15
  92.0 104.3 all-reduce.11
  371.7 64.2 all-reduce.13
  440.8 104.3 all-reduce.9
where the time goes:
time: 726 us; the launch traced here: 719 us
  waiting for transfers between devices  297 us (41%)
  other arithmetic  268 us (37%)
  matrix products  69.1 us (10%)
  local copies, waits for them, and re-layouts  65 us (9%)
  between operations  20.1 us (3%)
    psum x2, waiting for transfers between devices, per_device(): columns = lax.psum(mine_cols, 'col')  193 us
    another operation x29, other arithmetic, per_device(): factor = jnp.linalg.cholesky(pivot)  158 us
    psum x2, waiting for transfers between devices, per_device(): panel_rows, slab_rows = lax.psum((mine_rows, mine_slab), 'row')  104 us
    another operation x5, other arithmetic, solve_pivot(): lax.linalg.triangular_solve(factor, half, left_side=True, lower=True, tra...  79.2 us
    dot_general x4, matrix products, contract_rows(): lax.dot_general(gains, rows, (((0,), (0,)), ((), ())), precision=lax.Prec...  33.4 us
    another operation x14, matrix products, solve_pivot(): half = lax.linalg.triangular_solve(factor, rhs, left_side=True, lower=True)  18.3 us
    another operation x27, local copies, waits for them, and re-layouts, solve_pivot(): lax.linalg.triangular_solve(factor, half, left_side=True, lower=True, tra...  15.6 us
    another operation x4, other arithmetic, locate(): jnp.zeros((count,), jnp.float32).at[clipped].max(valid.astype(jnp.float32))  15.5 us
  transfers between devices with their start and end apart: 4, of which 4 were waited for; matrix products, arithmetic and copies ran while one was open for 6% of the time, Pallas kernels for 0%

commit v1 on v0

--- a/solution.py
+++ b/solution.py
@@ -47,7 +47,11 @@
         pivot = lax.psum(panel_pivot, "col")
         factor = jnp.linalg.cholesky(pivot)
         mine_cols = jnp.where(col_valid[None, :], jnp.take(inverse, col_pick, axis=1), 0.0)
-        columns = lax.psum(mine_cols, "col")
+        devs = lax.axis_size("col")
+        columns = mine_cols
+        for t in [[(b, b ^ ix) for b in range(devs)] for ix in (1, 2, 4, 8, 16) if ix < devs]:
+            base_arr = lax.ppermute(columns, "col", t)
+            columns = columns + base_arr
         gains = solve_pivot(factor, columns.T)
         slab = slab - contract_rows(gains, slab_rows)
         slab = jnp.where(row_marked[:, None], 0.0, slab)

time: 726 us -> 910 us (1.25)
  waiting for transfers between devices: 297 us -> 414 us
  other arithmetic: 268 us -> 303 us
  starting transfers between devices: 0.16 us -> 13 us
  local copies, waits for them, and re-layouts: 65 us -> 76.5 us
    ppermute x0 -> x8, waiting for transfers between devices: none -> 235 us  [per_device(): base_arr = lax.ppermute(columns, 'col', t)]
    psum x2, waiting for transfers between devices: 104 us -> 19.5 us  [per_device(): panel_rows, slab_rows = lax.psum((mine_rows, mine_slab), 'row')]
    psum x2, waiting for transfers between devices: 193 us -> 160 us  [per_device(): pivot = lax.psum(panel_pivot, 'col')]
    add x0 -> x6, other arithmetic: none -> 21.5 us  [per_device(): columns = columns + base_arr]
    ppermute x0 -> x8, starting transfers between devices: none -> 12.8 us  [per_device(): base_arr = lax.ppermute(columns, 'col', t)]
  transfers between devices with their start and end apart: 4 -> 12, of which waited for: 4 -> 8; matrix products, arithmetic and copies ran while one was open for 6% -> 39% of each run, Pallas kernels for 0% -> 0%
where the time goes in v1:
time: 910 us; the launch traced here: 900 us
  waiting for transfers between devices  414 us (45%)
  other arithmetic  303 us (33%)
  local copies, waits for them, and re-layouts  76.5 us (8%)
  matrix products  71.6 us (8%)
  between operations  20.1 us (2%)
  starting transfers between devices  13 us (1%)
    ppermute x8, waiting for transfers between devices, per_device(): base_arr = lax.ppermute(columns, 'col', t)  235 us
    another operation x29, other arithmetic, per_device(): factor = jnp.linalg.cholesky(pivot)  161 us
    psum x2, waiting for transfers between devices, per_device(): pivot = lax.psum(panel_pivot, 'col')  160 us
    another operation x5, other arithmetic, solve_pivot(): lax.linalg.triangular_solve(factor, half, left_side=True, lower=True, tra...  84.9 us
    dot_general x4, matrix products, contract_rows(): lax.dot_general(gains, rows, (((0,), (0,)), ((), ())), precision=lax.Prec...  34.9 us
    another operation x27, local copies, waits for them, and re-layouts, solve_pivot(): lax.linalg.triangular_solve(factor, half, left_side=True, lower=True, tra...  23.2 us
    add x6, other arithmetic, per_device(): columns = columns + base_arr  21.5 us
    psum x2, waiting for transfers between devices, per_device(): panel_rows, slab_rows = lax.psum((mine_rows, mine_slab), 'row')  19.5 us
  transfers between devices with their start and end apart: 12, of which 8 were waited for; matrix products, arithmetic and copies ran while one was open for 39% of the time, Pallas kernels for 0%

profile of v1, /device:TPU:1, one launch (start us, length us, event | category | flops | bytes accessed | tf_op | source)
XLA Modules:
  0.0 899.6 jit_solution(8846509649391553234)
XLA Ops:
  8.8 6.0 copy.13
  14.9 6.0 gather_fusion.2
  23.5 67.5 %collective-permute-done = f32[1536,512]{0,1:T(8,128)S(1)} collective-permute-done((f32[1536,512]{0,1:T(8,128)S(1)}, f32[1536,512]{0,1:T(8,128)S(1)}, u32[]{:S(2)}, u32[]{:S(2)}) %collective-permute-start) | collective-permute-done | bytes 3145760 | tf_op jit(solution)/shard_map/ppermute | solution.py:53
  93.1 3.1 collective-permute-start.1
  96.3 4.8 gather_fusion
  108.1 55.2 %collective-permute-done.1 = f32[1536,512]{0,1:T(8,128)} collective-permute-done((f32[1536,512]{0,1:T(8,128)}, f32[1536,512]{0,1:T(8,128)}, u32[]{:S(2)}, u32[]{:S(2)}) %collective-permute-start.1) | collective-permute-done | bytes 3145760 | tf_op jit(solution)/shard_map/ppermute | solution.py:53
  163.4 5.1 add.137
  169.6 5.0 all-reduce.14.cloned.1.call-done
  179.5 4.1 scatter_custom_fusion.3
  183.6 3.7 scatter_custom_fusion.2
  187.4 79.9 %all-reduce.8.cloned.1.call-done = f32[512,512]{0,1:T(8,128)} async-done(((f32[512,512]{0,1:T(8,128)}), f32[512,512]{0,1:T(8,128)}) %all-reduce.8.cloned.1.call-update) | async-done | bytes 1048592 | tf_op jit(solution)/shard_map/psum | solution.py:47
  270.3 11.7 %cholesky.286 = f32[128,128]{1,0:T(8,128)S(1)} custom-call(f32[128,128]{1,0:T(8,128)S(1)} %cholesky.426), custom_call_target="Cholesky" | custom-call | tf_op jit(solution)/shard_map/jit(cholesky)/cholesky | solution.py:48
  282.2 9.8 %custom-call.31 = f32[1,128,128]{1,2,0:T(8,128)S(1)} custom-call(f32[1,128,128]{2,1,0:T(8,128)S(1)} %get-tuple-element.96), custom_call_target="InvertDiagBlocksLowerTriangular" | custom-call | tf_op jit(solution)/shard_map/jit(cholesky)/cholesky | solution.py:48
  292.7 11.7 %cholesky.305 = f32[128,128]{1,0:T(8,128)S(1)} custom-call(f32[128,128]{1,0:T(8,128)S(1)} %cholesky.430), custom_call_target="Cholesky" | custom-call | tf_op jit(solution)/shard_map/jit(cholesky)/cholesky | solution.py:48
  304.4 10.2 %custom-call.32 = f32[1,128,128]{1,2,0:T(8,128)S(1)} custom-call(f32[1,128,128]{2,1,0:T(8,128)S(1)} %get-tuple-element.93), custom_call_target="InvertDiagBlocksLowerTriangular" | custom-call | tf_op jit(solution)/shard_map/jit(cholesky)/cholesky | solution.py:48
  314.6 3.4 add.138
  321.3 11.7 %cholesky.326 = f32[128,128]{1,0:T(8,128)S(1)} custom-call(f32[128,128]{1,0:T(8,128)S(1)} %cholesky.435), custom_call_target="Cholesky" | custom-call | tf_op jit(solution)/shard_map/jit(cholesky)/cholesky | solution.py:48
  333.7 9.8 %custom-call.33 = f32[1,128,128]{1,2,0:T(8,128)S(1)} custom-call(f32[1,128,128]{2,1,0:T(8,128)S(1)} %get-tuple-element.90), custom_call_target="InvertDiagBlocksLowerTriangular" | custom-call | tf_op jit(solution)/shard_map/jit(cholesky)/cholesky | solution.py:48
  345.7 11.7 %cholesky.343 = f32[128,128]{1,0:T(8,128)S(1)} custom-call(f32[128,128]{1,0:T(8,128)S(1)} %convolution_subtract_fusion.13), custom_call_target="Cholesky" | custom-call | tf_op jit(solution)/shard_map/jit(cholesky)/cholesky | solution.py:48
  364.9 12.1 %while.8 = (s32[]{:T(128)}, f32[512,512]{1,0:T(8,128)}, s32[4,2]{0,1:T(2,128)S(1)}, f32[4,128,128]{2,1,0:T(8,128)S(1)}, s32[]{:T(128)}) while((s32[]{:T(128)}, f32[512,512]{1,0:T(8,128)}, s32[4,2]{0,1:T(2,128)S(1)}, f32[4,128,128]{2,1,0:T(8,128)S(1)}, s32[]{:T(128)}) %tuple.80), condition=%wide.while_cond.1, body=%wide.while_body.1.sunk | while | flops 2 | bytes 131189 | solution.py:21
  377.7 40.1 %custom-call.35 = f32[4,128,128]{1,2,0:T(8,128)S(1)} custom-call(f32[4,128,128]{2,1,0:T(8,128)} %copy-done.18), custom_call_target="InvertDiagBlocksLowerTriangular" | custom-call | tf_op jit(solution)/shard_map/triangular_solve/custom-call.8 | solution.py:21
  417.8 2.6 add_bitcast_fusion.1
  434.9 10.7 %subtract_select_fusion.1 = f32[1536,768]{1,0:T(8,128)} fusion(f32[1536,768]{1,0:T(8,128)S(1)} %bitcast.161, f32[512,768]{1,0:T(8,128)S(1)} %copy-done.9, pred[768]{0:T(1024)(128)(4,1)S(1)} %broadcast_compare_fusion.2, pred[1536]{0:T(1024)(128)(4,1)S(1)} %broadcast_compare_fusion, f32[128,1536]{1,0:T(8,128)S(1)} %fusion.90, f32[128,1536]{1,0:T(8,128)S(1)} %fusion.89, ...), kind=kOutput, calls=%fused_computation.17 | convolution fusion | flops 7253655552 | bytes 14158080 | tf_op jit(solution)/shard_map/dot_general | solution.py:10
  445.6 6.0 copy.16
  451.6 6.0 gather_fusion.5
  458.9 65.7 %collective-permute-done.4 = f32[1536,512]{0,1:T(8,128)S(1)} collective-permute-done((f32[1536,512]{0,1:T(8,128)S(1)}, f32[1536,512]{0,1:T(8,128)S(1)}, u32[]{:S(2)}, u32[]{:S(2)}) %collective-permute-start.4) | collective-permute-done | bytes 3145760 | tf_op jit(solution)/shard_map/ppermute | solution.py:53
  529.2 6.1 gather_fusion.3
  535.3 7.0 fusion.1
  548.1 46.2 %collective-permute-done.5 = f32[1536,512]{0,1:T(8,128)} collective-permute-done((f32[1536,512]{0,1:T(8,128)}, f32[1536,512]{0,1:T(8,128)}, u32[]{:S(2)}, u32[]{:S(2)}) %collective-permute-start.5) | collective-permute-done | bytes 3145760 | tf_op jit(solution)/shard_map/ppermute | solution.py:53
  594.3 5.2 add.141
  600.8 14.5 %all-reduce.12.cloned.1.call-done = (f32[512,768]{1,0:T(8,128)}, f32[512,256]{1,0:T(8,128)}) async-done(((f32[512,768]{1,0:T(8,128)}, f32[512,256]{1,0:T(8,128)}), (f32[512,768]{1,0:T(8,128)}, f32[512,256]{1,0:T(8,128)})) %all-reduce.12.cloned.1.call-update) | async-done | bytes 2097168 | tf_op jit(solution)/shard_map/psum | solution.py:45
  620.0 4.1 scatter_custom_fusion.1
  624.1 3.7 scatter_custom_fusion
  627.8 80.3 %all-reduce.10.cloned.1.call-done = f32[512,512]{0,1:T(8,128)} async-done(((f32[512,512]{0,1:T(8,128)}), f32[512,512]{0,1:T(8,128)}) %all-reduce.10.cloned.1.call-update) | async-done | bytes 1048592 | tf_op jit(solution)/shard_map/psum | solution.py:47
  711.2 11.7 %cholesky.358 = f32[128,128]{1,0:T(8,128)S(1)} custom-call(f32[128,128]{1,0:T(8,128)S(1)} %cholesky.439), custom_call_target="Cholesky" | custom-call | tf_op jit(solution)/shard_map/jit(cholesky)/cholesky | solution.py:48
  723.1 9.8 %custom-call.36 = f32[1,128,128]{1,2,0:T(8,128)S(1)} custom-call(f32[1,128,128]{2,1,0:T(8,128)S(1)} %get-tuple-element.86), custom_call_target="InvertDiagBlocksLowerTriangular" | custom-call | tf_op jit(solution)/shard_map/jit(cholesky)/cholesky | solution.py:48
  733.6 11.7 %cholesky.377 = f32[128,128]{1,0:T(8,128)S(1)} custom-call(f32[128,128]{1,0:T(8,128)S(1)} %cholesky.443), custom_call_target="Cholesky" | custom-call | tf_op jit(solution)/shard_map/jit(cholesky)/cholesky | solution.py:48
  745.3 10.2 %custom-call.37 = f32[1,128,128]{1,2,0:T(8,128)S(1)} custom-call(f32[1,128,128]{2,1,0:T(8,128)S(1)} %get-tuple-element.83), custom_call_target="InvertDiagBlocksLowerTriangular" | custom-call | tf_op jit(solution)/shard_map/jit(cholesky)/cholesky | solution.py:48
  756.8 3.4 add.142
  762.5 11.7 %cholesky.398 = f32[128,128]{1,0:T(8,128)S(1)} custom-call(f32[128,128]{1,0:T(8,128)S(1)} %cholesky.448), custom_call_target="Cholesky" | custom-call | tf_op jit(solution)/shard_map/jit(cholesky)/cholesky | solution.py:48
  774.9 9.8 %custom-call.38 = f32[1,128,128]{1,2,0:T(8,128)S(1)} custom-call(f32[1,128,128]{2,1,0:T(8,128)S(1)} %get-tuple-element.80), custom_call_target="InvertDiagBlocksLowerTriangular" | custom-call | tf_op jit(solution)/shard_map/jit(cholesky)/cholesky | solution.py:48
  787.0 11.7 %cholesky.415 = f32[128,128]{1,0:T(8,128)S(1)} custom-call(f32[128,128]{1,0:T(8,128)S(1)} %convolution_subtract_fusion.12), custom_call_target="Cholesky" | custom-call | tf_op jit(solution)/shard_map/jit(cholesky)/cholesky | solution.py:48
  804.5 2.3 select_select_fusion.2
  806.9 11.6 %while.9 = (s32[]{:T(128)}, f32[512,512]{1,0:T(8,128)}, s32[4,2]{0,1:T(2,128)S(1)}, f32[4,128,128]{2,1,0:T(8,128)S(1)}, s32[]{:T(128)}) while((s32[]{:T(128)}, f32[512,512]{1,0:T(8,128)}, s32[4,2]{0,1:T(2,128)S(1)}, f32[4,128,128]{2,1,0:T(8,128)S(1)}, s32[]{:T(128)}) %tuple.96), condition=%wide.while_cond.1.clone, body=%wide.while_body.1.clone.sunk | while | flops 2 | bytes 131189 | solution.py:21
  819.2 40.1 %custom-call.40 = f32[4,128,128]{1,2,0:T(8,128)S(1)} custom-call(f32[4,128,128]{2,1,0:T(8,128)} %copy-done.17), custom_call_target="InvertDiagBlocksLowerTriangular" | custom-call | tf_op jit(solution)/shard_map/triangular_solve/custom-call.8 | solution.py:21
  859.4 2.6 add_bitcast_fusion
  875.6 10.7 %subtract_select_fusion = f32[1536,768]{1,0:T(8,128)} fusion(f32[1536,768]{1,0:T(8,128)S(1)} %bitcast.159, f32[512,768]{1,0:T(8,128)S(1)} %copy-done.10, pred[768]{0:T(1024)(128)(4,1)S(1)} %broadcast_compare_fusion.3, pred[1536]{0:T(1024)(128)(4,1)S(1)} %broadcast_compare_fusion.1, f32[128,1536]{1,0:T(8,128)S(1)} %fusion.94, f32[128,1536]{1,0:T(8,128)S(1)} %fusion.93, ...), kind=kOutput, calls=%fused_computation.16 | convolution fusion | flops 7253655552 | bytes 14158080 | tf_op jit(solution)/shard_map/dot_general | solution.py:10
  886.3 6.6 fusion.2
  (204 shorter events, 117.9 us)
Async XLA Ops:
  7.2 167.5 %all-reduce.14.cloned.1.call-start = ((), (), s32[]{:S(2)}) async-start(), calls=%async_computation.3 | async-start | bytes 4194304 | tf_op jit(solution)/shard_map/psum | solution.py:45
  21.3 69.7 %collective-permute-start = (f32[1536,512]{0,1:T(8,128)S(1)}, f32[1536,512]{0,1:T(8,128)S(1)}, u32[]{:S(2)}, u32[]{:S(2)}) collective-permute-start(f32[1536,512]{0,1:T(8,128)S(1)} %bitcast_select_fusion.1), channel_id=1, source_target_pairs={{0,1},{1,0},{2,3},{3,2},{4,5},{5,4},{6,7},{7,6},{8,9},{9,8},{10,11... | collective-permute-start | bytes 9437192 | tf_op jit(solution)/shard_map/ppermute | solution.py:53
  93.1 70.2 %collective-permute-start.1 = (f32[1536,512]{0,1:T(8,128)}, f32[1536,512]{0,1:T(8,128)}, u32[]{:S(2)}, u32[]{:S(2)}) collective-permute-start(f32[1536,512]{0,1:T(8,128)} %fusion.136), channel_id=1, source_target_pairs={{0,2},{1,3},{2,0},{3,1},{4,6},{5,7},{6,4},{7,5},{8,10},{9,11},{10,... | collective-permute-start | bytes 9437192 | tf_op jit(solution)/shard_map/ppermute | solution.py:53
  108.1 159.2 %all-reduce.8.cloned.1.call-start = ((), (), s32[]{:S(2)}) async-start(), calls=%async_computation | async-start | bytes 2097152 | tf_op jit(solution)/shard_map/psum | solution.py:47
  168.5 146.1 %collective-permute-start.2 = (f32[1536,512]{0,1:T(8,128)}, f32[1536,512]{0,1:T(8,128)}, u32[]{:S(2)}, u32[]{:S(2)}) collective-permute-start(f32[1536,512]{0,1:T(8,128)} %add.137), channel_id=1, source_target_pairs={{0,4},{1,5},{2,6},{3,7},{4,0},{5,1},{6,2},{7,3},{8,12},{9,13},{10,... | collective-permute-start | bytes 9437192 | tf_op jit(solution)/shard_map/ppermute | solution.py:53
  179.4 435.9 %all-reduce.12.cloned.1.call-start = ((), (), s32[]{:S(2)}) async-start(), calls=%async_computation.2 | async-start | bytes 4194304 | tf_op jit(solution)/shard_map/psum | solution.py:45
  270.3 44.3 %copy-start.15 = (f32[512,512]{1,0:T(8,128)}, f32[512,512]{1,0:T(8,128)S(1)}, u32[]{:S(2)}) copy-start(f32[512,512]{1,0:T(8,128)S(1)} %fusion.40) | copy-start | bytes 3145732
  304.4 10.2 %copy-start.7 = (f32[512,512]{1,0:T(8,128)}, f32[512,512]{1,0:T(8,128)S(1)}, u32[]{:S(2)}) copy-start(f32[512,512]{1,0:T(8,128)S(1)} %get-tuple-element.94) | copy-start | bytes 3145732
  318.1 99.7 %collective-permute-start.3 = (f32[1536,512]{0,1:T(8,128)S(1)}, f32[1536,512]{0,1:T(8,128)}, u32[]{:S(2)}, u32[]{:S(2)}) collective-permute-start(f32[1536,512]{0,1:T(8,128)S(1)} %add.138), channel_id=1, source_target_pairs={{0,8},{1,9},{2,10},{3,11},{4,12},{5,13},{6,14},{7,15},{8,0},{9,1},... | collective-permute-start | bytes 9437192 | tf_op jit(solution)/shard_map/ppermute | solution.py:53
  376.9 0.7 copy-start.18
  417.8 3.4 copy-start.13
  426.3 8.7 slice-start.2
  427.9 6.1 copy-start
  429.6 4.5 copy-start.2
  429.6 5.3 slice-start.3
  431.4 2.6 copy-start.6
  431.4 3.5 copy-start.9
  434.0 0.9 copy-start.14
  458.0 66.6 %collective-permute-start.4 = (f32[1536,512]{0,1:T(8,128)S(1)}, f32[1536,512]{0,1:T(8,128)S(1)}, u32[]{:S(2)}, u32[]{:S(2)}) collective-permute-start(f32[1536,512]{0,1:T(8,128)S(1)} %bitcast_select_fusion), channel_id=1, source_target_pairs={{0,1},{1,0},{2,3},{3,2},{4,5},{5,4},{6,7},{7,6},{8,9},{9,8},{10,11... | collective-permute-start | bytes 9437192 | tf_op jit(solution)/shard_map/ppermute | solution.py:53
  526.9 67.5 %collective-permute-start.5 = (f32[1536,512]{0,1:T(8,128)}, f32[1536,512]{0,1:T(8,128)}, u32[]{:S(2)}, u32[]{:S(2)}) collective-permute-start(f32[1536,512]{0,1:T(8,128)} %fusion.135), channel_id=1, source_target_pairs={{0,2},{1,3},{2,0},{3,1},{4,6},{5,7},{6,4},{7,5},{8,10},{9,11},{10,... | collective-permute-start | bytes 9437192 | tf_op jit(solution)/shard_map/ppermute | solution.py:53
  529.2 6.1 copy-start.1
  529.2 6.1 copy-start.3
  542.3 5.7 copy-start.4
  542.3 4.3 copy-start.11
  548.0 160.1 %all-reduce.10.cloned.1.call-start = ((), (), s32[]{:S(2)}) async-start(), calls=%async_computation.1 | async-start | bytes 2097152 | tf_op jit(solution)/shard_map/psum | solution.py:47
  599.5 157.2 %collective-permute-start.6 = (f32[1536,512]{0,1:T(8,128)}, f32[1536,512]{0,1:T(8,128)}, u32[]{:S(2)}, u32[]{:S(2)}) collective-permute-start(f32[1536,512]{0,1:T(8,128)} %add.141), channel_id=1, source_target_pairs={{0,4},{1,5},{2,6},{3,7},{4,0},{5,1},{6,2},{7,3},{8,12},{9,13},{10,... | collective-permute-start | bytes 9437192 | tf_op jit(solution)/shard_map/ppermute | solution.py:53
  711.2 44.6 %copy-start.16 = (f32[512,512]{1,0:T(8,128)}, f32[512,512]{1,0:T(8,128)S(1)}, u32[]{:S(2)}) copy-start(f32[512,512]{1,0:T(8,128)S(1)} %fusion.39) | copy-start | bytes 3145732
  755.8 1.0 copy-start.8
  760.2 99.2 %collective-permute-start.7 = (f32[1536,512]{0,1:T(8,128)S(1)}, f32[1536,512]{0,1:T(8,128)}, u32[]{:S(2)}, u32[]{:S(2)}) collective-permute-start(f32[1536,512]{0,1:T(8,128)S(1)} %add.142), channel_id=1, source_target_pairs={{0,8},{1,9},{2,10},{3,11},{4,12},{5,13},{6,14},{7,15},{8,0},{9,1},... | collective-permute-start | bytes 9437192 | tf_op jit(solution)/shard_map/ppermute | solution.py:53
  818.5 0.7 copy-start.17
  859.3 3.4 copy-start.12
  867.8 7.7 slice-start
  871.1 4.4 slice-start.1
  872.9 2.6 copy-start.10
  875.6 10.7 %copy-start.5 = (f32[1536,256]{1,0:T(8,128)S(1)}, f32[1536,256]{1,0:T(8,128)}, u32[]{:S(2)}) copy-start(f32[1536,256]{1,0:T(8,128)} %copy-done.4) | copy-start | bytes 4718596
  875.6 10.7 %copy-start.19 = (f32[512,256]{1,0:T(8,128)S(1)}, f32[512,256]{1,0:T(8,128)}, u32[]{:S(2)}) copy-start(f32[512,256]{1,0:T(8,128)} %get-tuple-element.62) | copy-start | bytes 1572868
Sparse Core Ops, SparseCore 0:
  108.2 66.4 all-reduce.13
  179.5 87.7 all-reduce.7
  548.2 67.0 all-reduce.11
  620.1 87.9 all-reduce.9
